TPU v7x, 32 devices: a whole 2x2x4 slice. The times are simulated.
32 devices in a mesh: batch: 8 (over z, y), wide: 4 (over x, core).
Axes of the slice: x: 2, y: 2, z: 4, core: 2. Of those that a mesh axis runs over, the one named last changes fastest.
Arguments:
- tokens: bfloat16 [16384, 768], P(('batch', 'wide')), may hold values from -6 to 6
- block_row: int32 [128], P(('batch', 'wide')), may hold values from 0 to 3, as said below
- block_live: int32 [128], P(('batch', 'wide')), may hold values from 0 to 128, as said below
- query_weight: float32 [768, 768], P(('batch', 'wide')), may hold values from -0.21875 to 0.21875
- key_weight: float32 [768, 768], P(('batch', 'wide')), may hold values from -0.21875 to 0.21875
- value_weight: float32 [768, 768], P(('batch', 'wide')), may hold values from -0.21875 to 0.21875
- out_weight: float32 [768, 768], P(('batch', 'wide')), may hold values from -2.5 to 2.5
- position_bias: float32 [12, 1024], replicated, may hold values from -3 to 3
- features: float32 [64, 64], replicated, may hold values from -5 to 5
- up_weight: float32 [768, 3072], P('batch', 'wide'), may hold values from -0.21875 to 0.21875
- up_bias: float32 [3072], replicated, may hold values from -1.5 to 1.5
- down_weight: float32 [768, 3072], P('batch', 'wide'), may hold values from -0.109375 to 0.109375
- down_bias: float32 [768], replicated, may hold values from -1.5 to 1.5
- gain_one: float32 [768], replicated, may hold values from 0.5 to 1.5
- shift_one: float32 [768], replicated, may hold values from -1 to 1
- gain_two: float32 [768], replicated, may hold values from 0.5 to 1.5
- shift_two: float32 [768], replicated, may hold values from -1 to 1
- cotangent: bfloat16 [16384, 768], P(('batch', 'wide')), may hold values from -6 to 6
Outputs:
- out_tokens: bfloat16 [16384, 768], P(('batch', 'wide'))
- grad_tokens: float32 [16384, 768], P(('batch', 'wide'))
- grad_query_weight: float32 [768, 768], P(('batch', 'wide'))
- grad_key_weight: float32 [768, 768], P(('batch', 'wide'))
- grad_value_weight: float32 [768, 768], P(('batch', 'wide'))
- grad_out_weight: float32 [768, 768], P(('batch', 'wide'))
- grad_position_bias: float32 [12, 1024], replicated
- grad_up_weight: float32 [768, 3072], P('batch', 'wide')
- grad_up_bias: float32 [3072], replicated
- grad_down_weight: float32 [768, 3072], P('batch', 'wide')
- grad_down_bias: float32 [768], replicated
- grad_gain_one: float32 [768], replicated
- grad_shift_one: float32 [768], replicated
- grad_gain_two: float32 [768], replicated
- grad_shift_two: float32 [768], replicated
Inputs may be any that keep to these rules, and one draw needn't show every extreme that they name: `block_row`: in each device's 512 // 128 entries the row numbers start at 0 and rise by one at the first block of each row; a row covers an aligned run of a power of two blocks, from one block to all of a device's blocks. `block_live`: the live tokens of a row are its first ones and more than half of its blocks' slots; a one-block row is full.
All inputs are finite; a program needn't handle non-finite values.
Results may differ from a plain program's by a relative error of at most 0.018.
Values may be sent and summed in bfloat16 or wider, within the bound.
No kernel may reach another device: no remote copies, remote signals or barrier semaphores. Data moves between devices by JAX's collectives and lax.ppermute only.
A program may use at most 192 MiB of HBM per device.

v0:
```python
from functools import partial
import jax
import jax.numpy as jnp
from jax import lax
from jax.sharding import PartitionSpec as P

BLK = 128
eps = 1e-05
highest = lax.Precision.HIGHEST
rows_contract = (((0,), (0,)), ((), ()))
cols_contract = (((1,), (1,)), ((), ()))


def token_masks(block_row, block_live, width):
    blocks = block_row.shape[0]
    offsets = jnp.broadcast_to(jnp.arange(width, dtype=jnp.int32)[None, :], (blocks, width))
    row_ids = jnp.broadcast_to(block_row[:, None], (blocks, width)).reshape(-1)
    live_tok = (offsets < block_live[:, None]).astype(jnp.float32).reshape(-1)
    return (row_ids, live_tok)


def toeplitz_from(vector, length):
    flipped = vector[::-1]
    tiled_flat = jnp.broadcast_to(flipped[None, :], (length, 2 * length)).reshape(-1)
    return tiled_flat[: length * (2 * length - 1)].reshape(length, 2 * length - 1)[:, length - 1 :]


def diagonal_sums(matrix, length):
    padded = jnp.concatenate([jnp.zeros((length, length), jnp.float32), matrix], axis=1).reshape(-1)
    padded = jnp.concatenate([padded, jnp.zeros((length,), jnp.float32)])
    column_sums = jnp.sum(padded.reshape(length, 2 * length + 1), axis=0)
    return column_sums[::-1][: 2 * length]


def feature_map(head_part, features):
    scaled = head_part * head_part.shape[-1] ** (-0.25)
    projected = jnp.einsum("thd,df->thf", scaled, features, precision=highest)
    return jnp.exp(projected - 0.5 * jnp.sum(scaled * scaled, axis=-1, keepdims=True))


def layer_norm(residual, scale_row, shift_row):
    centered = residual - jnp.mean(residual, axis=-1, keepdims=True)
    variance = jnp.mean(centered * centered, axis=-1, keepdims=True)
    return centered * lax.rsqrt(variance + eps) * scale_row + shift_row


def exact_gelu(hidden):
    return jax.nn.gelu(hidden, approximate=False)


def attend_head(same_row, query_phi, key_phi, bias_row):
    length = query_phi.shape[0]
    scores = jnp.einsum("if,jf->ij", query_phi, key_phi, preferred_element_type=jnp.float32)
    coupling = toeplitz_from(jnp.exp(bias_row), length) * same_row
    weights = coupling * scores
    totals = jnp.sum(weights, axis=1, keepdims=True)
    return (weights, totals, coupling)


def mix_head(same_row, head_in):
    query_phi, key_phi, value_head, bias_row = head_in
    weights, totals, coupling = attend_head(same_row, query_phi, key_phi, bias_row)
    prob_low = (weights / totals).astype(jnp.bfloat16)
    return jnp.einsum("ij,jd->id", prob_low, value_head, preferred_element_type=jnp.float32)


def head_backward(same_row, head_in):
    query_phi, key_phi, value_head, bias_row, grad_mix = head_in
    length = query_phi.shape[0]
    weights, totals, coupling = attend_head(same_row, query_phi, key_phi, bias_row)
    shares = weights / totals
    prob_low = shares.astype(jnp.bfloat16)
    grad_probs = jnp.einsum("id,jd->ij", grad_mix, value_head, preferred_element_type=jnp.float32)
    grad_value = jnp.einsum("ij,id->jd", prob_low, grad_mix, preferred_element_type=jnp.float32)
    inner_sum = jnp.sum(grad_probs * shares, axis=1, keepdims=True)
    grad_weights = (grad_probs - inner_sum) / totals
    grad_bias = diagonal_sums(grad_weights * weights, length)
    grad_scores = (grad_weights * coupling).astype(jnp.bfloat16)
    grad_query_phi = jnp.einsum(
        "ij,jf->if", grad_scores, key_phi, preferred_element_type=jnp.float32
    )
    grad_key_phi = jnp.einsum(
        "ij,if->jf", grad_scores, query_phi, preferred_element_type=jnp.float32
    )
    return (grad_query_phi, grad_key_phi, grad_value, grad_bias)


def per_device(
    tokens,
    block_row,
    block_live,
    query_weight,
    key_weight,
    value_weight,
    out_weight,
    position_bias,
    features,
    up_weight,
    up_bias,
    down_weight,
    down_bias,
    gain_one,
    shift_one,
    gain_two,
    shift_two,
    cotangent,
):
    length = tokens.shape[0]
    head_count = position_bias.shape[0]
    head_size = features.shape[0]
    head_shape = (length, head_count, head_size)
    row_ids, live_tok = token_masks(block_row, block_live, BLK)
    same_row = (row_ids[:, None] == row_ids[None, :]).astype(jnp.float32) * live_tok[None, :]
    query_full, key_full, value_full, out_full = (
        lax.all_gather(query_weight.astype(jnp.bfloat16), ("batch", "wide"), axis=0, tiled=True),
        lax.all_gather(key_weight.astype(jnp.bfloat16), ("batch", "wide"), axis=0, tiled=True),
        lax.all_gather(value_weight.astype(jnp.bfloat16), ("batch", "wide"), axis=0, tiled=True),
        lax.all_gather(out_weight.astype(jnp.bfloat16), ("batch", "wide"), axis=0, tiled=True),
    )
    up_rows, down_rows = (
        lax.all_gather(up_weight.astype(jnp.bfloat16), "batch", axis=0, tiled=True),
        lax.all_gather(down_weight.astype(jnp.bfloat16), "batch", axis=0, tiled=True),
    )
    queries = jnp.dot(tokens, query_full, preferred_element_type=jnp.float32)
    key_rows = jnp.dot(tokens, key_full, preferred_element_type=jnp.float32)
    values = jnp.dot(tokens, value_full, preferred_element_type=jnp.float32).astype(jnp.bfloat16)
    map_features = partial(feature_map, features=features)
    query_map, query_back = jax.vjp(map_features, queries.reshape(head_shape))
    key_map, key_back = jax.vjp(map_features, key_rows.reshape(head_shape))
    query_phi = jnp.swapaxes(query_map.astype(jnp.bfloat16), 0, 1)
    key_phi = jnp.swapaxes(key_map.astype(jnp.bfloat16), 0, 1)
    value_heads = jnp.swapaxes(values.reshape(head_shape), 0, 1)
    mixed_heads = lax.map(
        partial(mix_head, same_row), (query_phi, key_phi, value_heads, position_bias)
    )
    mixed_low = jnp.swapaxes(mixed_heads, 0, 1).reshape(length, -1).astype(jnp.bfloat16)
    attention = jnp.dot(mixed_low, out_full, preferred_element_type=jnp.float32)
    residual_one = tokens.astype(jnp.float32) + attention
    normed_one, norm_one_back = jax.vjp(layer_norm, residual_one, gain_one, shift_one)
    normed_low = normed_one.astype(jnp.bfloat16)
    wide_index = lax.axis_index("wide")
    hidden_width = up_rows.shape[1]
    bias_part = lax.dynamic_slice_in_dim(up_bias, wide_index * hidden_width, hidden_width, 0)
    group_rows = lax.all_gather(normed_low, "wide", axis=0, tiled=True)
    hidden = jnp.dot(group_rows, up_rows, preferred_element_type=jnp.float32) + bias_part
    activation_full, gelu_back = jax.vjp(exact_gelu, hidden)
    activation = activation_full.astype(jnp.bfloat16)
    block_rows = activation
    branch = (
        lax.psum_scatter(
            lax.dot_general(
                block_rows, down_rows, cols_contract, preferred_element_type=jnp.float32
            ).astype(jnp.bfloat16),
            "wide",
            scatter_dimension=0,
            tiled=True,
        ).astype(jnp.float32)
        + down_bias
    )
    residual_two = normed_one + branch
    normed_two, norm_two_back = jax.vjp(layer_norm, residual_two, gain_two, shift_two)
    out_tokens = (normed_two * live_tok[:, None]).astype(jnp.bfloat16)
    grad_out = cotangent.astype(jnp.float32) * live_tok[:, None]
    grad_two, grad_gain_two, grad_shift_two = norm_two_back(grad_out)
    grad_branch = grad_two.astype(jnp.bfloat16)
    grad_down_bias = jnp.sum(grad_branch, axis=0, dtype=jnp.float32)
    group_grads = lax.all_gather(grad_branch, "wide", axis=0, tiled=True)
    grad_act = jnp.dot(group_grads, down_rows, preferred_element_type=jnp.float32)
    grad_hidden = gelu_back(grad_act)[0].astype(jnp.bfloat16)
    grad_up_part = lax.dot_general(
        group_rows, grad_hidden, rows_contract, preferred_element_type=jnp.float32
    )
    grad_down_part = lax.dot_general(
        group_grads, activation, rows_contract, preferred_element_type=jnp.float32
    )
    bias_sum = jnp.sum(grad_hidden, axis=0, dtype=jnp.float32)
    bias_grad = lax.dynamic_update_slice_in_dim(
        jnp.zeros(up_bias.shape, jnp.float32), bias_sum, wide_index * hidden_width, 0
    )
    block_rows = grad_hidden
    grad_back = lax.psum_scatter(
        lax.dot_general(
            block_rows, up_rows, cols_contract, preferred_element_type=jnp.float32
        ).astype(jnp.bfloat16),
        "wide",
        scatter_dimension=0,
        tiled=True,
    ).astype(jnp.float32)
    grad_back, grad_up_part, grad_down_part, grad_up_bias = (
        grad_back,
        grad_up_part,
        grad_down_part,
        bias_grad,
    )
    grad_up_weight, grad_down_weight = (
        lax.psum_scatter(
            grad_up_part.astype(jnp.bfloat16), "batch", scatter_dimension=0, tiled=True
        ).astype(jnp.float32),
        lax.psum_scatter(
            grad_down_part.astype(jnp.bfloat16), "batch", scatter_dimension=0, tiled=True
        ).astype(jnp.float32),
    )
    grad_one, grad_gain_one, grad_shift_one = norm_one_back(grad_two + grad_back)
    grad_attention = grad_one.astype(jnp.bfloat16)
    grad_out_local = lax.dot_general(
        mixed_low, grad_attention, rows_contract, preferred_element_type=jnp.float32
    )
    grad_mixed = lax.dot_general(
        grad_attention, out_full, cols_contract, preferred_element_type=jnp.float32
    ).astype(jnp.bfloat16)
    grad_mixed_heads = jnp.swapaxes(grad_mixed.reshape(head_shape), 0, 1)
    grad_query_phi, grad_key_phi, grad_value_heads, grad_bias_local = lax.map(
        partial(head_backward, same_row),
        (query_phi, key_phi, value_heads, position_bias, grad_mixed_heads),
    )
    grad_queries = (
        query_back(jnp.swapaxes(grad_query_phi, 0, 1))[0].reshape(length, -1).astype(jnp.bfloat16)
    )
    grad_keys = (
        key_back(jnp.swapaxes(grad_key_phi, 0, 1))[0].reshape(length, -1).astype(jnp.bfloat16)
    )
    grad_values = jnp.swapaxes(grad_value_heads, 0, 1).reshape(length, -1).astype(jnp.bfloat16)
    grad_query_local = lax.dot_general(
        tokens, grad_queries, rows_contract, preferred_element_type=jnp.float32
    )
    grad_key_local = lax.dot_general(
        tokens, grad_keys, rows_contract, preferred_element_type=jnp.float32
    )
    grad_value_local = lax.dot_general(
        tokens, grad_values, rows_contract, preferred_element_type=jnp.float32
    )
    grad_query_weight, grad_key_weight, grad_value_weight, grad_out_weight = (
        lax.psum_scatter(grad_query_local, ("batch", "wide"), scatter_dimension=0, tiled=True),
        lax.psum_scatter(grad_key_local, ("batch", "wide"), scatter_dimension=0, tiled=True),
        lax.psum_scatter(grad_value_local, ("batch", "wide"), scatter_dimension=0, tiled=True),
        lax.psum_scatter(grad_out_local, ("batch", "wide"), scatter_dimension=0, tiled=True),
    )
    grad_tokens = (
        grad_one
        + lax.dot_general(
            grad_queries, query_full, cols_contract, preferred_element_type=jnp.float32
        )
        + lax.dot_general(grad_keys, key_full, cols_contract, preferred_element_type=jnp.float32)
        + lax.dot_general(
            grad_values, value_full, cols_contract, preferred_element_type=jnp.float32
        )
    )
    (
        grad_up_bias,
        grad_down_bias,
        grad_gain_one,
        grad_shift_one,
        grad_gain_two,
        grad_shift_two,
        grad_position_bias,
    ) = lax.psum(
        (
            grad_up_bias,
            grad_down_bias,
            grad_gain_one,
            grad_shift_one,
            grad_gain_two,
            grad_shift_two,
            grad_bias_local,
        ),
        ("batch", "wide"),
    )
    return (
        out_tokens,
        grad_tokens,
        grad_query_weight,
        grad_key_weight,
        grad_value_weight,
        grad_out_weight,
        grad_position_bias,
        grad_up_weight,
        grad_up_bias,
        grad_down_weight,
        grad_down_bias,
        grad_gain_one,
        grad_shift_one,
        grad_gain_two,
        grad_shift_two,
    )


def solution(mesh):
    placed = (
        P(("batch", "wide"), None),
        P(("batch", "wide")),
        P(("batch", "wide")),
        P(("batch", "wide"), None),
        P(("batch", "wide"), None),
        P(("batch", "wide"), None),
        P(("batch", "wide"), None),
        P(),
        P(),
        P("batch", "wide"),
        P(),
        P("batch", "wide"),
        P(),
        P(),
        P(),
        P(),
        P(),
        P(("batch", "wide"), None),
    )
    return jax.shard_map(
        per_device,
        mesh=mesh,
        in_specs=placed,
        out_specs=(
            P(("batch", "wide"), None),
            P(("batch", "wide"), None),
            P(("batch", "wide"), None),
            P(("batch", "wide"), None),
            P(("batch", "wide"), None),
            P(("batch", "wide"), None),
            P(),
            P("batch", "wide"),
            P(),
            P("batch", "wide"),
            P(),
            P(),
            P(),
            P(),
            P(),
        ),
        check_vma=False,
    )
```

profile of v0, /device:TPU:0, one launch (start us, length us, event | category | flops | bytes accessed | tf_op | source)
XLA Modules:
  0.0 1346.2 jit_solution(8290527931595110936)
XLA Ops:
  16.6 51.7 %all-gather.11.cloned.1.call-done = bf16[768,768]{1,0:T(8,128)(2,1)} async-done(((bf16[24,768]{1,0:T(8,128)(2,1)}), bf16[768,768]{1,0:T(8,128)(2,1)}) %all-gather.11.cloned.1.call-update) | async-done | bytes 1179664 | tf_op jit(solution)/shard_map/all_gather | solution.py:116
  68.3 3.7 broadcast_multiply_fusion
  74.7 3.2 fusion.46
  80.4 44.4 %all-gather.9.cloned.1.call-done = bf16[768,768]{1,0:T(8,128)(2,1)} async-done(((bf16[24,768]{1,0:T(8,128)(2,1)}), bf16[768,768]{1,0:T(8,128)(2,1)}) %all-gather.9.cloned.1.call-update) | async-done | bytes 1179664 | tf_op jit(solution)/shard_map/all_gather | solution.py:115
  124.7 3.8 broadcast_multiply_fusion.1
  131.3 3.2 fusion.48
  137.0 44.3 %all-gather.13.cloned.1.call-done = bf16[768,768]{1,0:T(8,128)(2,1)} async-done(((bf16[24,768]{1,0:T(8,128)(2,1)}), bf16[768,768]{1,0:T(8,128)(2,1)}) %all-gather.13.cloned.1.call-update) | async-done | bytes 1179664 | tf_op jit(solution)/shard_map/all_gather | solution.py:117
  185.1 113.5 %while.30 = (s32[]{:T(128)}, bf16[12,512,64]{1,2,0:T(8,128)(2,1)}, f32[12,1024]{1,0:T(8,128)}, bf16[12,512,64]{2,1,0:T(8,128)(2,1)}, bf16[12,512,64]{2,1,0:T(8,1...) while((s32[]{:T(128)}, bf16[12,512,64]{1,2,0:T(8,128)(2,1)}, ...), condition=%wide.region_4.5_spmd.clone.clone, body=%wide.region_2.4_spmd.clone.sunk.clone | while | flops 68943360 | bytes 18378840 | solution.py:133
  186.7 2.8 reshape.224
  196.1 2.8 reshape.224
  205.6 2.8 reshape.224
  215.0 2.8 reshape.224
  224.5 2.8 reshape.224
  234.0 2.8 reshape.224
  243.4 2.8 reshape.224
  252.9 2.8 reshape.224
  262.3 2.8 reshape.224
  271.8 2.8 reshape.224
  281.3 2.8 reshape.224
  290.7 2.8 reshape.224
  304.7 25.9 %all-gather.17.cloned.1.call-done = bf16[2048,768]{1,0:T(8,128)(2,1)} async-done(((bf16[512,768]{1,0:T(8,128)(2,1)}), bf16[2048,768]{1,0:T(8,128)(2,1)}) %all-gather.17.cloned.1.call-update) | async-done | bytes 3145744 | tf_op jit(solution)/shard_map/all_gather | solution.py:144
  330.6 18.9 %multiply_convert_fusion.1 = (bf16[2048,768]{1,0:T(8,128)(2,1)}, f32[2048,768]{1,0:T(8,128)}, f32[2048,768]{1,0:T(8,128)}) fusion(f32[768]{0:T(1024)S(1)} %dynamic_slice.32, bf16[2048,768]{1,0:T(8,128)(2,1)} %all-gather.17.cloned.1.call-done, bf16[768,768]{1,0:T(8,128)(2,1)} %all-gather.19.cloned.1.call-done), kind=kOutput, calls=%fused_computation.59 | convolution fusion | flops 2519728128 | bytes 20057088 | tf_op jit(solution)/shard_map/dot_general | solution.py:145
  349.5 25.0 %all-gather.21.cloned.1.call-done = bf16[768,768]{1,0:T(8,128)(2,1)} async-done(((bf16[96,768]{1,0:T(8,128)(2,1)}), bf16[768,768]{1,0:T(8,128)(2,1)}) %all-gather.21.cloned.1.call-update) | async-done | bytes 1179664 | tf_op jit(solution)/shard_map/all_gather | solution.py:122
  374.4 6.5 convolution_convert_fusion.1
  381.1 36.8 %reduce-scatter.15.cloned.1.call-done = bf16[512,768]{1,0:T(8,128)(2,1)} async-done(((bf16[2048,768]{1,0:T(8,128)(2,1)}), bf16[512,768]{1,0:T(8,128)(2,1)}) %reduce-scatter.15.cloned.1.call-update) | async-done | bytes 786448 | tf_op jit(solution)/shard_map/reduce_scatter | solution.py:150
  425.8 28.4 %all-gather.23.cloned.1.call-done = bf16[2048,768]{1,0:T(8,128)(2,1)} async-done(((bf16[512,768]{1,0:T(8,128)(2,1)}), bf16[2048,768]{1,0:T(8,128)(2,1)}) %all-gather.23.cloned.1.call-update) | async-done | bytes 3145744 | tf_op jit(solution)/shard_map/all_gather | solution.py:167
  454.2 10.6 convert_reduce_fusion
  466.4 4.0 convolution_convert_fusion
  470.5 6.5 convolution_convert_fusion.2
  477.5 7.4 convolution_convert_fusion.3
  485.3 23.3 %reduce-scatter.17.cloned.1.call-done = bf16[512,768]{1,0:T(8,128)(2,1)} async-done(((bf16[2048,768]{1,0:T(8,128)(2,1)}), bf16[512,768]{1,0:T(8,128)(2,1)}) %reduce-scatter.17.cloned.1.call-update) | async-done | bytes 786448 | tf_op jit(solution)/shard_map/reduce_scatter | solution.py:181
  515.3 272.2 %while.31 = (s32[]{:T(128)}, f32[12,512,64]{1,2,0:T(8,128)}, f32[12,512,64]{1,2,0:T(8,128)}, bf16[12,512,64]{1,2,0:T(8,128)(2,1)}, f32[12,1024]{1,0:T(8,128)}, /...) while((s32[]{:T(128)}, f32[12,512,64]{1,2,0:T(8,128)}, ...), condition=%wide.region_19.20_spmd.clone.clone, body=%wide.region_15.0_spmd.clone.sunk.clone | while | flops 173013504 | bytes 51068068 | solution.py:212
  516.9 2.8 reshape.225
  527.3 3.2 reshape.226
  539.6 2.8 reshape.225
  550.0 3.2 reshape.226
  562.3 2.8 reshape.225
  572.8 3.2 reshape.226
  585.0 2.8 reshape.225
  595.4 3.2 reshape.226
  607.7 2.8 reshape.225
  618.2 3.2 reshape.226
  630.4 2.8 reshape.225
  640.8 3.2 reshape.226
  653.1 2.8 reshape.225
  663.5 3.2 reshape.226
  675.8 2.8 reshape.225
  686.2 3.2 reshape.226
  708.8 3.2 reshape.226
  731.5 3.2 reshape.226
  754.2 3.2 reshape.226
  776.9 3.2 reshape.226
  787.6 4.0 fusion.68
  791.9 3.1 copy.80
  795.0 3.5 fusion.56
  804.0 3.1 copy.94
  807.1 3.0 copy.86
  810.1 3.9 fusion.50
  821.0 3.1 copy.98
  833.1 78.5 %all-reduce.5.cloned.1.call-done = (f32[12,1024]{1,0:T(8,128)}, f32[3072]{0:T(1024)}, f32[768]{0:T(1024)}, f32[768]{0:T(1024)}, f32[768]{0:T(1024)}, /*index=5*/f32[768]{0:T(1024)}, f32[768]{0:T(1024)}) async-done(((f32[12,1024]{1,0:T(8,128)}, f32[3072]{0:T(1024)}, f32[768]{0:T(1024)}, f32[768]{0:T(1024)}, f32[768]{0:T(1024)}, /*index=5*/f32[768]{0:T(1024)}, f32[768]{0:T(1024)}), (f32[12,1024]{1,0:T(8,128)}, ...) | async-done | bytes 76816 | tf_op jit(solution)/shard_map/psum | solution.py:256
  911.5 105.9 %reduce-scatter.19.cloned.1.call-done = f32[24,768]{1,0:T(8,128)} async-done(((f32[768,768]{1,0:T(8,128)}), f32[24,768]{1,0:T(8,128)}) %reduce-scatter.19.cloned.1.call-update) | async-done | bytes 73744 | tf_op jit(solution)/shard_map/reduce_scatter | solution.py:236
  1017.5 104.5 %reduce-scatter.25.cloned.1.call-done = f32[24,768]{1,0:T(8,128)} async-done(((f32[768,768]{1,0:T(8,128)}), f32[24,768]{1,0:T(8,128)}) %reduce-scatter.25.cloned.1.call-update) | async-done | bytes 73744
  1122.0 103.8 %reduce-scatter.27.cloned.1.call-done = f32[24,768]{1,0:T(8,128)} async-done(((f32[768,768]{1,0:T(8,128)}), f32[24,768]{1,0:T(8,128)}) %reduce-scatter.27.cloned.1.call-update) | async-done | bytes 73744
  1225.8 104.5 %reduce-scatter.29.cloned.1.call-done = f32[24,768]{1,0:T(8,128)} async-done(((f32[768,768]{1,0:T(8,128)}), f32[24,768]{1,0:T(8,128)}) %reduce-scatter.29.cloned.1.call-update) | async-done | bytes 73744
  (536 shorter events, 367.7 us)
Async XLA Ops:
  7.2 67.6 %copy-start = (f32[64,64]{1,0:T(8,128)S(1)}, f32[64,64]{1,0:T(8,128)}, u32[]{:S(2)}) copy-start(f32[64,64]{1,0:T(8,128)} %param.30) | copy-start | bytes 49156
  7.2 8.2 copy-start.30
  7.2 61.1 %all-gather.11.cloned.1.call-start = ((), (), s32[]{:S(2)}) async-start(), calls=%async_computation.9 | async-start | bytes 1216512 | tf_op jit(solution)/shard_map/all_gather | solution.py:116
  8.8 116.0 %all-gather.9.cloned.1.call-start = ((), (), s32[]{:S(2)}) async-start(), calls=%async_computation.8 | async-start | bytes 1216512 | tf_op jit(solution)/shard_map/all_gather | solution.py:115
  10.4 170.9 %all-gather.13.cloned.1.call-start = ((), (), s32[]{:S(2)}) async-start(), calls=%async_computation.10 | async-start | bytes 1216512 | tf_op jit(solution)/shard_map/all_gather | solution.py:117
  11.9 4.6 copy-start.31
  11.9 56.4 %copy-start.2 = (bf16[512,768]{1,0:T(8,128)(2,1)S(1)}, bf16[512,768]{1,0:T(8,128)(2,1)}, u32[]{:S(2)}) copy-start(bf16[512,768]{1,0:T(8,128)(2,1)} %param.22) | copy-start | bytes 2359300
  12.0 286.7 %all-gather.15.cloned.1.call-start = ((), (), s32[]{:S(2)}) async-start(), calls=%async_computation.11 | async-start | bytes 1216512 | tf_op jit(solution)/shard_map/all_gather | solution.py:118
  13.6 291.1 %all-gather.19.cloned.1.call-start = ((), (), s32[]{:S(2)}) async-start(), calls=%async_computation.13 | async-start | bytes 1327104 | tf_op jit(solution)/shard_map/all_gather | solution.py:121
  15.3 315.3 %all-gather.17.cloned.1.call-start = ((), (), s32[]{:S(2)}) async-start(), calls=%async_computation.12 | async-start | bytes 3932160 | tf_op jit(solution)/shard_map/all_gather | solution.py:144
  15.4 56.6 %copy-start.8 = (bf16[12,512,64]{1,2,0:T(8,128)(2,1)}, bf16[12,512,64]{1,2,0:T(8,128)(2,1)S(1)}, u32[]{:S(2)}) copy-start(bf16[12,512,64]{1,2,0:T(8,128)(2,1)S(1)} %fusion.76) | copy-start | bytes 2359300
  301.0 0.7 copy-start.24
  301.0 0.7 copy-start.26
  301.7 1.3 copy-start.23
  302.9 71.5 %all-gather.21.cloned.1.call-start = ((), (), s32[]{:S(2)}) async-start(), calls=%async_computation.14 | async-start | bytes 1327104 | tf_op jit(solution)/shard_map/all_gather | solution.py:122
  303.7 114.2 %reduce-scatter.15.cloned.1.call-start = ((), (), s32[]{:S(2)}) async-start(), calls=%async_computation.15 | async-start | bytes 3932160 | tf_op jit(solution)/shard_map/reduce_scatter | solution.py:150
  381.0 36.9 %copy-start.28 = (f32[768]{0:T(1024)S(1)}, f32[768]{0:T(1024)}, u32[]{:S(2)}) copy-start(f32[768]{0:T(1024)} %param.34) | copy-start | bytes 9220
  381.0 73.2 %all-gather.23.cloned.1.call-start = ((), (), s32[]{:S(2)}) async-start(), calls=%async_computation.16 | async-start | bytes 3932160 | tf_op jit(solution)/shard_map/all_gather | solution.py:167
  419.6 1.1 copy-start.12
  419.6 1.1 copy-start.27
  420.0 2.1 copy-start.29
  425.5 83.1 %reduce-scatter.17.cloned.1.call-start = ((), (), s32[]{:S(2)}) async-start(), calls=%async_computation.17 | async-start | bytes 3932160 | tf_op jit(solution)/shard_map/reduce_scatter | solution.py:181
  454.2 12.3 copy-start.33
  464.8 1.7 copy-start.34
  470.5 353.7 %reduce-scatter.23.cloned.1.call-start = ((), (), s32[]{:S(2)}) async-start(), calls=%async_computation.20 | async-start | bytes 1327104 | tf_op jit(solution)/shard_map/reduce_scatter | solution.py:199
  477.1 348.9 %reduce-scatter.21.cloned.1.call-start = ((), (), s32[]{:S(2)}) async-start(), calls=%async_computation.19 | async-start | bytes 1327104 | tf_op jit(solution)/shard_map/reduce_scatter | solution.py:196
  477.5 7.4 copy-start.25
  484.9 426.7 %all-reduce.5.cloned.1.call-start = ((), (), s32[]{:S(2)}) async-start(), calls=%async_computation.24 | async-start | bytes 196608 | tf_op jit(solution)/shard_map/psum | solution.py:256
  508.6 2.6 copy-start.13
  511.2 2.1 copy-start.32
  512.1 1.2 copy-start.4
  523.0 1.4 copy-start.1
  545.7 1.5 copy-start.1
  568.4 1.4 copy-start.1
  591.1 1.4 copy-start.1
  613.8 1.4 copy-start.1
  636.5 1.5 copy-start.1
  659.2 1.5 copy-start.1
  681.9 1.4 copy-start.1
  704.5 1.4 copy-start.1
  727.2 1.4 copy-start.1
  749.9 1.4 copy-start.1
  772.5 1.5 copy-start.1
  787.5 229.9 %reduce-scatter.19.cloned.1.call-start = ((), (), s32[]{:S(2)}) async-start(), calls=%async_computation.18 | async-start | bytes 2433024 | tf_op jit(solution)/shard_map/reduce_scatter | solution.py:236
  791.6 330.4 %reduce-scatter.25.cloned.1.call-start = ((), (), s32[]{:S(2)}) async-start(), calls=%async_computation.21 | async-start | bytes 2433024
  791.8 3.2 copy-start.6
  791.8 3.2 copy-start.21
  791.8 3.1 copy-start.22
  795.0 3.5 copy-start.7
  795.0 3.5 copy-start.10
  795.0 3.8 copy-start.11
  798.8 2.9 copy-start.3
  800.8 0.9 copy-start.14
  807.0 418.8 %reduce-scatter.27.cloned.1.call-start = ((), (), s32[]{:S(2)}) async-start(), calls=%async_computation.22 | async-start | bytes 2433024
  814.0 0.9 copy-start.16
  817.7 1.1 copy-start.9
  817.7 512.6 %reduce-scatter.29.cloned.1.call-start = ((), (), s32[]{:S(2)}) async-start(), calls=%async_computation.23 | async-start | bytes 2433024
  824.1 3.5 copy-start.15
  824.1 3.5 copy-start.20
  827.6 1.1 copy-start.17
  827.6 1.5 copy-start.19
  829.1 1.4 copy-start.5
  829.1 1.8 copy-start.18
Sparse Core Ops, SparseCore 0:
  11.5 56.7 all-gather.10
  71.7 52.9 all-gather.8
  128.2 52.9 all-gather.12
  184.6 52.9 all-gather.14
  240.2 39.9 all-gather.18
  303.1 27.4 all-gather.16
  333.3 41.0 all-gather.20
  381.1 36.7 reduce-scatter.14
  425.6 28.5 all-gather.22
  470.6 37.9 reduce-scatter.16
  512.0 64.1 reduce-scatter.22
  579.4 63.0 reduce-scatter.20
  787.7 123.8 all-reduce.4
  917.3 100.1 reduce-scatter.18
  1024.0 97.9 reduce-scatter.24
  1127.7 98.0 reduce-scatter.26
  1232.4 97.9 reduce-scatter.28
where the time goes:
time: 1360 us; the launch traced here: 1350 us
  waiting for transfers between devices  777 us (57%)
  local copies, waits for them, and re-layouts  285 us (21%)
  matrix products  231 us (17%)
  other arithmetic  34.5 us (3%)
  between operations  14.6 us (1%)
    unnamed x20, waiting for transfers between devices  313 us
    reduce_scatter x1, waiting for transfers between devices, per_device(): lax.psum_scatter(grad_out_local, ('batch', 'wide'), scatter_dimension=0,...  106 us
    psum x1, waiting for transfers between devices, per_device(): lax.psum((grad_up_bias, grad_down_bias, grad_gain_one, grad_shift_one, gr...  78.5 us
    reshape x24, local copies, waits for them, and re-layouts, toeplitz_from(): tiled_flat[:length * (2 * length - 1)].reshape(length, 2 * length - 1)  66.9 us
    all_gather x1, waiting for transfers between devices, per_device(): lax.all_gather(key_weight.astype(jnp.bfloat16), ('batch', 'wide'), axis=0...  51.7 us
    all_gather x1, waiting for transfers between devices, per_device(): lax.all_gather(query_weight.astype(jnp.bfloat16), ('batch', 'wide'), axis...  44.4 us
    all_gather x1, waiting for transfers between devices, per_device(): lax.all_gather(value_weight.astype(jnp.bfloat16), ('batch', 'wide'), axis...  44.3 us
    slice x24, local copies, waits for them, and re-layouts, toeplitz_from(): tiled_flat[:length * (2 * length - 1)].reshape(length, 2 * length - 1)  39.7 us
  transfers between devices with their start and end apart: 17, of which 13 were waited for; matrix products, arithmetic and copies ran while one was open for 37% of the time, Pallas kernels for 0%

commit v1 on v0

--- a/solution.py
+++ b/solution.py
@@ -3,6 +3,7 @@
 import jax.numpy as jnp
 from jax import lax
 from jax.sharding import PartitionSpec as P
+from jax.lax import psum
 
 BLK = 128
 eps = 1e-05
@@ -245,6 +246,12 @@
             grad_values, value_full, cols_contract, preferred_element_type=jnp.float32
         )
     )
+
+    def _remake_space(xs):
+        for num in ("wide", "batch"):
+            xs = psum(xs, num)
+        return xs
+
     (
         grad_up_bias,
         grad_down_bias,
@@ -253,7 +260,7 @@
         grad_gain_two,
         grad_shift_two,
         grad_position_bias,
-    ) = lax.psum(
+    ) = _remake_space(
         (
             grad_up_bias,
             grad_down_bias,
@@ -262,8 +269,7 @@
             grad_gain_two,
             grad_shift_two,
             grad_bias_local,
-        ),
-        ("batch", "wide"),
+        )
     )
     return (
         out_tokens,

time: 1360 us -> 1480 us (1.088)
  waiting for transfers between devices: 777 us -> 892 us
    reduce_scatter x1, waiting for transfers between devices: 0.01 us -> 65.2 us  [per_device(): lax.psum_scatter(grad_up_part.astype(jnp.bfloat16), 'batch', scatter_dime...]
    reduce_scatter x1, waiting for transfers between devices: 0.02 us -> 29.3 us  [per_device(): lax.psum_scatter(grad_down_part.astype(jnp.bfloat16), 'batch', scatter_di...]
    psum x1 -> x2, waiting for transfers between devices: 78.5 us -> 86 us  [_remake_space(): xs = psum(xs, num)]
    unnamed x20 -> x21, waiting for transfers between devices: 313 us -> 313 us
    unnamed x82 -> x80, local copies, waits for them, and re-layouts: 33.6 us -> 33.5 us
  transfers between devices with their start and end apart: 17 -> 18, of which waited for: 13 -> 16; matrix products, arithmetic and copies ran while one was open for 37% -> 16% of each run, Pallas kernels for 0% -> 0%
where the time goes in v1:
time: 1480 us; the launch traced here: 1460 us
  waiting for transfers between devices  892 us (60%)
  local copies, waits for them, and re-layouts  285 us (19%)
  matrix products  232 us (16%)
  other arithmetic  34.9 us (2%)
  between operations  15.2 us (1%)
    unnamed x21, waiting for transfers between devices  313 us
    reduce_scatter x1, waiting for transfers between devices, per_device(): lax.psum_scatter(grad_out_local, ('batch', 'wide'), scatter_dimension=0,...  105 us
    psum x2, waiting for transfers between devices, _remake_space(): xs = psum(xs, num)  86 us
    reshape x24, local copies, waits for them, and re-layouts, toeplitz_from(): tiled_flat[:length * (2 * length - 1)].reshape(length, 2 * length - 1)  67.1 us
    reduce_scatter x1, waiting for transfers between devices, per_device(): lax.psum_scatter(grad_up_part.astype(jnp.bfloat16), 'batch', scatter_dime...  65.2 us
    all_gather x1, waiting for transfers between devices, per_device(): lax.all_gather(key_weight.astype(jnp.bfloat16), ('batch', 'wide'), axis=0...  51.7 us
    all_gather x1, waiting for transfers between devices, per_device(): lax.all_gather(query_weight.astype(jnp.bfloat16), ('batch', 'wide'), axis...  44.4 us
    all_gather x1, waiting for transfers between devices, per_device(): lax.all_gather(value_weight.astype(jnp.bfloat16), ('batch', 'wide'), axis...  44.3 us
  transfers between devices with their start and end apart: 18, of which 16 were waited for; matrix products, arithmetic and copies ran while one was open for 16% of the time, Pallas kernels for 0%

profile of v1, /device:TPU:0, one launch (start us, length us, event | category | flops | bytes accessed | tf_op | source)
XLA Modules:
  0.0 1463.1 jit_solution(5220341674289912776)
XLA Ops:
  16.6 51.7 %all-gather.11.cloned.1.call-done = bf16[768,768]{1,0:T(8,128)(2,1)} async-done(((bf16[24,768]{1,0:T(8,128)(2,1)}), bf16[768,768]{1,0:T(8,128)(2,1)}) %all-gather.11.cloned.1.call-update) | async-done | bytes 1179664 | tf_op jit(solution)/shard_map/all_gather | solution.py:117
  68.3 3.7 broadcast_multiply_fusion
  74.8 3.2 fusion.46
  80.4 44.4 %all-gather.9.cloned.1.call-done = bf16[768,768]{1,0:T(8,128)(2,1)} async-done(((bf16[24,768]{1,0:T(8,128)(2,1)}), bf16[768,768]{1,0:T(8,128)(2,1)}) %all-gather.9.cloned.1.call-update) | async-done | bytes 1179664 | tf_op jit(solution)/shard_map/all_gather | solution.py:116
  124.7 3.8 broadcast_multiply_fusion.1
  131.3 3.2 fusion.48
  137.0 44.3 %all-gather.13.cloned.1.call-done = bf16[768,768]{1,0:T(8,128)(2,1)} async-done(((bf16[24,768]{1,0:T(8,128)(2,1)}), bf16[768,768]{1,0:T(8,128)(2,1)}) %all-gather.13.cloned.1.call-update) | async-done | bytes 1179664 | tf_op jit(solution)/shard_map/all_gather | solution.py:118
  185.1 113.5 %while.30 = (s32[]{:T(128)}, bf16[12,512,64]{1,2,0:T(8,128)(2,1)}, f32[12,1024]{1,0:T(8,128)}, bf16[12,512,64]{2,1,0:T(8,128)(2,1)}, bf16[12,512,64]{2,1,0:T(8,1...) while((s32[]{:T(128)}, bf16[12,512,64]{1,2,0:T(8,128)(2,1)}, ...), condition=%wide.region_4.5_spmd.clone.clone, body=%wide.region_2.4_spmd.clone.sunk.clone | while | flops 68943360 | bytes 18378840 | solution.py:134
  186.7 2.8 reshape.224
  196.1 2.8 reshape.224
  205.6 2.8 reshape.224
  215.0 2.8 reshape.224
  243.4 2.8 reshape.224
  304.9 25.7 %all-gather.17.cloned.1.call-done = bf16[2048,768]{1,0:T(8,128)(2,1)} async-done(((bf16[512,768]{1,0:T(8,128)(2,1)}), bf16[2048,768]{1,0:T(8,128)(2,1)}) %all-gather.17.cloned.1.call-update) | async-done | bytes 3145744 | tf_op jit(solution)/shard_map/all_gather | solution.py:145
  330.6 18.9 %multiply_convert_fusion.1 = (bf16[2048,768]{1,0:T(8,128)(2,1)}, f32[2048,768]{1,0:T(8,128)}, f32[2048,768]{1,0:T(8,128)}) fusion(f32[768]{0:T(1024)S(1)} %dynamic_slice.32, bf16[2048,768]{1,0:T(8,128)(2,1)} %all-gather.17.cloned.1.call-done, bf16[768,768]{1,0:T(8,128)(2,1)} %all-gather.19.cloned.1.call-done), kind=kOutput, calls=%fused_computation.59 | convolution fusion | flops 2519728128 | bytes 20057088 | tf_op jit(solution)/shard_map/dot_general | solution.py:146
  349.5 25.0 %all-gather.21.cloned.1.call-done = bf16[768,768]{1,0:T(8,128)(2,1)} async-done(((bf16[96,768]{1,0:T(8,128)(2,1)}), bf16[768,768]{1,0:T(8,128)(2,1)}) %all-gather.21.cloned.1.call-update) | async-done | bytes 1179664 | tf_op jit(solution)/shard_map/all_gather | solution.py:123
  374.4 6.6 convolution_convert_fusion.1
  381.1 36.8 %reduce-scatter.15.cloned.1.call-done = bf16[512,768]{1,0:T(8,128)(2,1)} async-done(((bf16[2048,768]{1,0:T(8,128)(2,1)}), bf16[512,768]{1,0:T(8,128)(2,1)}) %reduce-scatter.15.cloned.1.call-update) | async-done | bytes 786448 | tf_op jit(solution)/shard_map/reduce_scatter | solution.py:151
  425.5 28.6 %all-gather.23.cloned.1.call-done = bf16[2048,768]{1,0:T(8,128)(2,1)} async-done(((bf16[512,768]{1,0:T(8,128)(2,1)}), bf16[2048,768]{1,0:T(8,128)(2,1)}) %all-gather.23.cloned.1.call-update) | async-done | bytes 3145744 | tf_op jit(solution)/shard_map/all_gather | solution.py:168
  454.2 10.6 convert_reduce_fusion
  466.4 4.1 convolution_convert_fusion
  471.1 37.5 %reduce-scatter.17.cloned.1.call-done = bf16[512,768]{1,0:T(8,128)(2,1)} async-done(((bf16[2048,768]{1,0:T(8,128)(2,1)}), bf16[512,768]{1,0:T(8,128)(2,1)}) %reduce-scatter.17.cloned.1.call-update) | async-done | bytes 786448 | tf_op jit(solution)/shard_map/reduce_scatter | solution.py:182
  515.3 272.7 %while.31 = (s32[]{:T(128)}, f32[12,512,64]{1,2,0:T(8,128)}, f32[12,512,64]{1,2,0:T(8,128)}, bf16[12,512,64]{1,2,0:T(8,128)(2,1)}, f32[12,1024]{1,0:T(8,128)}, /...) while((s32[]{:T(128)}, f32[12,512,64]{1,2,0:T(8,128)}, ...), condition=%wide.region_19.20_spmd.clone.clone, body=%wide.region_15.0_spmd.clone.sunk.clone | while | flops 173013504 | bytes 51068068 | solution.py:213
  516.8 2.8 reshape.225
  527.3 3.2 reshape.226
  539.5 2.8 reshape.225
  550.0 3.2 reshape.226
  562.3 2.8 reshape.225
  572.7 3.2 reshape.226
  585.0 2.8 reshape.225
  595.4 3.2 reshape.226
  607.7 2.8 reshape.225
  618.1 3.2 reshape.226
  630.4 2.8 reshape.225
  640.9 3.2 reshape.226
  653.1 2.8 reshape.225
  663.6 3.2 reshape.226
  675.9 2.8 reshape.225
  686.3 3.2 reshape.226
  698.6 2.8 reshape.225
  709.0 3.2 reshape.226
  721.3 2.8 reshape.225
  731.7 3.2 reshape.226
  744.0 2.8 reshape.225
  754.5 3.2 reshape.226
  766.8 2.8 reshape.225
  777.2 3.2 reshape.226
  788.2 6.5 convolution_convert_fusion.2
  794.8 6.6 convolution_convert_fusion.3
  801.5 18.6 %all-reduce.9.cloned.1.call-done = (f32[12,1024]{1,0:T(8,128)}, f32[3072]{0:T(1024)}, f32[768]{0:T(1024)}, f32[768]{0:T(1024)}, f32[768]{0:T(1024)}, /*index=5*/f32[768]{0:T(1024)}, f32[768]{0:T(1024)}) async-done(((f32[12,1024]{1,0:T(8,128)}, f32[3072]{0:T(1024)}, f32[768]{0:T(1024)}, f32[768]{0:T(1024)}, f32[768]{0:T(1024)}, /*index=5*/f32[768]{0:T(1024)}, f32[768]{0:T(1024)}), (f32[12,1024]{1,0:T(8,128)}, ...) | async-done | bytes 76816 | tf_op jit(solution)/shard_map/psum | solution.py:252
  822.6 3.0 copy.80
  825.7 3.9 fusion.56
  835.1 3.1 copy.94
  838.5 3.0 copy.86
  841.6 4.4 fusion.50
  849.1 3.1 copy.96
  855.5 3.1 copy.98
  858.6 29.3 %reduce-scatter.23.cloned.1.call-done = bf16[96,768]{1,0:T(8,128)(2,1)} async-done(((bf16[768,768]{1,0:T(8,128)(2,1)}), bf16[96,768]{1,0:T(8,128)(2,1)}) %reduce-scatter.23.cloned.1.call-update) | async-done | bytes 147472 | tf_op jit(solution)/shard_map/reduce_scatter | solution.py:200
  889.6 65.2 %reduce-scatter.21.cloned.1.call-done = bf16[96,768]{1,0:T(8,128)(2,1)} async-done(((bf16[768,768]{1,0:T(8,128)(2,1)}), bf16[96,768]{1,0:T(8,128)(2,1)}) %reduce-scatter.21.cloned.1.call-update) | async-done | bytes 147472 | tf_op jit(solution)/shard_map/reduce_scatter | solution.py:197
  962.2 67.4 %all-reduce.7.cloned.1.call-done = (f32[12,1024]{1,0:T(8,128)}, f32[3072]{0:T(1024)}, f32[768]{0:T(1024)}, f32[768]{0:T(1024)}, f32[768]{0:T(1024)}, /*index=5*/f32[768]{0:T(1024)}, f32[768]{0:T(1024)}) async-done(((f32[12,1024]{1,0:T(8,128)}, f32[3072]{0:T(1024)}, f32[768]{0:T(1024)}, f32[768]{0:T(1024)}, f32[768]{0:T(1024)}, /*index=5*/f32[768]{0:T(1024)}, f32[768]{0:T(1024)}), (f32[12,1024]{1,0:T(8,128)}, ...) | async-done | bytes 76816 | tf_op jit(solution)/shard_map/psum | solution.py:252
  1029.6 104.7 %reduce-scatter.19.cloned.1.call-done = f32[24,768]{1,0:T(8,128)} async-done(((f32[768,768]{1,0:T(8,128)}), f32[24,768]{1,0:T(8,128)}) %reduce-scatter.19.cloned.1.call-update) | async-done | bytes 73744 | tf_op jit(solution)/shard_map/reduce_scatter | solution.py:237
  1134.4 103.8 %reduce-scatter.25.cloned.1.call-done = f32[24,768]{1,0:T(8,128)} async-done(((f32[768,768]{1,0:T(8,128)}), f32[24,768]{1,0:T(8,128)}) %reduce-scatter.25.cloned.1.call-update) | async-done | bytes 73744
  1238.1 104.6 %reduce-scatter.27.cloned.1.call-done = f32[24,768]{1,0:T(8,128)} async-done(((f32[768,768]{1,0:T(8,128)}), f32[24,768]{1,0:T(8,128)}) %reduce-scatter.27.cloned.1.call-update) | async-done | bytes 73744
  1342.8 103.9 %reduce-scatter.29.cloned.1.call-done = f32[24,768]{1,0:T(8,128)} async-done(((f32[768,768]{1,0:T(8,128)}), f32[24,768]{1,0:T(8,128)}) %reduce-scatter.29.cloned.1.call-update) | async-done | bytes 73744
  (537 shorter events, 378.3 us)
Async XLA Ops:
  7.2 67.6 %copy-start = (f32[64,64]{1,0:T(8,128)S(1)}, f32[64,64]{1,0:T(8,128)}, u32[]{:S(2)}) copy-start(f32[64,64]{1,0:T(8,128)} %param.30) | copy-start | bytes 49156
  7.2 8.2 copy-start.29
  7.2 61.1 %all-gather.11.cloned.1.call-start = ((), (), s32[]{:S(2)}) async-start(), calls=%async_computation.9 | async-start | bytes 1216512 | tf_op jit(solution)/shard_map/all_gather | solution.py:117
  8.8 116.0 %all-gather.9.cloned.1.call-start = ((), (), s32[]{:S(2)}) async-start(), calls=%async_computation.8 | async-start | bytes 1216512 | tf_op jit(solution)/shard_map/all_gather | solution.py:116
  10.4 170.9 %all-gather.13.cloned.1.call-start = ((), (), s32[]{:S(2)}) async-start(), calls=%async_computation.10 | async-start | bytes 1216512 | tf_op jit(solution)/shard_map/all_gather | solution.py:118
  11.9 4.6 copy-start.30
  11.9 56.4 %copy-start.2 = (bf16[512,768]{1,0:T(8,128)(2,1)S(1)}, bf16[512,768]{1,0:T(8,128)(2,1)}, u32[]{:S(2)}) copy-start(bf16[512,768]{1,0:T(8,128)(2,1)} %param.22) | copy-start | bytes 2359300
  12.0 286.7 %all-gather.15.cloned.1.call-start = ((), (), s32[]{:S(2)}) async-start(), calls=%async_computation.11 | async-start | bytes 1216512 | tf_op jit(solution)/shard_map/all_gather | solution.py:119
  13.6 291.3 %all-gather.19.cloned.1.call-start = ((), (), s32[]{:S(2)}) async-start(), calls=%async_computation.13 | async-start | bytes 1327104 | tf_op jit(solution)/shard_map/all_gather | solution.py:122
  15.3 315.3 %all-gather.17.cloned.1.call-start = ((), (), s32[]{:S(2)}) async-start(), calls=%async_computation.12 | async-start | bytes 3932160 | tf_op jit(solution)/shard_map/all_gather | solution.py:145
  15.4 56.6 %copy-start.7 = (bf16[12,512,64]{1,2,0:T(8,128)(2,1)}, bf16[12,512,64]{1,2,0:T(8,128)(2,1)S(1)}, u32[]{:S(2)}) copy-start(bf16[12,512,64]{1,2,0:T(8,128)(2,1)S(1)} %fusion.76) | copy-start | bytes 2359300
  301.0 0.7 copy-start.23
  301.1 0.7 copy-start.25
  301.8 1.3 copy-start.22
  303.0 71.5 %all-gather.21.cloned.1.call-start = ((), (), s32[]{:S(2)}) async-start(), calls=%async_computation.14 | async-start | bytes 1327104 | tf_op jit(solution)/shard_map/all_gather | solution.py:123
  303.7 114.1 %reduce-scatter.15.cloned.1.call-start = ((), (), s32[]{:S(2)}) async-start(), calls=%async_computation.15 | async-start | bytes 3932160 | tf_op jit(solution)/shard_map/reduce_scatter | solution.py:151
  381.0 36.9 %copy-start.27 = (f32[768]{0:T(1024)S(1)}, f32[768]{0:T(1024)}, u32[]{:S(2)}) copy-start(f32[768]{0:T(1024)} %param.34) | copy-start | bytes 9220
  381.0 73.2 %all-gather.23.cloned.1.call-start = ((), (), s32[]{:S(2)}) async-start(), calls=%async_computation.16 | async-start | bytes 3932160 | tf_op jit(solution)/shard_map/all_gather | solution.py:168
  419.6 1.1 copy-start.12
  419.6 1.1 copy-start.26
  419.9 2.1 copy-start.28
  425.5 83.1 %reduce-scatter.17.cloned.1.call-start = ((), (), s32[]{:S(2)}) async-start(), calls=%async_computation.17 | async-start | bytes 3932160 | tf_op jit(solution)/shard_map/reduce_scatter | solution.py:182
  454.2 12.2 copy-start.32
  464.7 1.6 copy-start.33
  470.5 349.6 %all-reduce.9.cloned.1.call-start = ((), (), s32[]{:S(2)}) async-start(), calls=%async_computation.25 | async-start | bytes 196608 | tf_op jit(solution)/shard_map/psum | solution.py:252
  471.0 40.2 %copy-start.24 = (f32[3072]{0:T(1024)}, f32[3072]{0:T(1024)S(1)}, u32[]{:S(2)}) copy-start(f32[3072]{0:T(1024)S(1)} %dynamic_update_slice.20) | copy-start | bytes 36868
  508.6 2.6 copy-start.13
  511.2 2.0 copy-start.31
  512.1 1.2 copy-start.4
  523.0 1.4 copy-start.1
  545.7 1.4 copy-start.1
  568.4 1.4 copy-start.1
  591.1 1.4 copy-start.1
  613.8 1.4 copy-start.1
  636.5 1.5 copy-start.1
  659.3 1.4 copy-start.1
  682.0 1.4 copy-start.1
  704.7 1.5 copy-start.1
  727.4 1.5 copy-start.1
  750.2 1.5 copy-start.1
  772.9 1.5 copy-start.1
  788.0 100.0 %reduce-scatter.23.cloned.1.call-start = ((), (), s32[]{:S(2)}) async-start(), calls=%async_computation.20 | async-start | bytes 1327104 | tf_op jit(solution)/shard_map/reduce_scatter | solution.py:200
  794.8 160.0 %reduce-scatter.21.cloned.1.call-start = ((), (), s32[]{:S(2)}) async-start(), calls=%async_computation.19 | async-start | bytes 1327104 | tf_op jit(solution)/shard_map/reduce_scatter | solution.py:197
  794.8 25.4 %copy-start.5 = (f32[512,768]{1,0:T(8,128)S(1)}, f32[512,768]{1,0:T(8,128)}, u32[]{:S(2)}) copy-start(f32[512,768]{1,0:T(8,128)} %copy-done.4) | copy-start | bytes 4718596
  801.5 18.7 %copy-start.11 = (bf16[12,512,64]{1,2,0:T(8,128)(2,1)S(1)}, bf16[12,512,64]{1,2,0:T(8,128)(2,1)}, u32[]{:S(2)}) copy-start(bf16[12,512,64]{1,2,0:T(8,128)(2,1)} %get-tuple-element.112) | copy-start | bytes 2359300
  801.5 228.1 %all-reduce.7.cloned.1.call-start = ((), (), s32[]{:S(2)}) async-start(), calls=%async_computation.24 | async-start | bytes 196608 | tf_op jit(solution)/shard_map/psum | solution.py:252
  820.1 314.2 %reduce-scatter.19.cloned.1.call-start = ((), (), s32[]{:S(2)}) async-start(), calls=%async_computation.18 | async-start | bytes 2433024 | tf_op jit(solution)/shard_map/reduce_scatter | solution.py:237
  822.5 415.6 %reduce-scatter.25.cloned.1.call-start = ((), (), s32[]{:S(2)}) async-start(), calls=%async_computation.21 | async-start | bytes 2433024
  822.6 3.1 copy-start.20
  822.6 3.1 copy-start.21
  825.7 4.0 copy-start.6
  825.7 4.0 copy-start.9
  825.7 4.2 copy-start.10
  829.9 3.0 copy-start.3
  831.9 1.0 copy-start.14
  838.2 504.5 %reduce-scatter.27.cloned.1.call-start = ((), (), s32[]{:S(2)}) async-start(), calls=%async_computation.22 | async-start | bytes 2433024
  846.0 0.9 copy-start.16
  852.2 1.1 copy-start.8
  852.2 594.5 %reduce-scatter.29.cloned.1.call-start = ((), (), s32[]{:S(2)}) async-start(), calls=%async_computation.23 | async-start | bytes 2433024
  858.6 97.8 %copy-start.15 = (bf16[512,12,64]{0,2,1:T(8,128)(2,1)S(1)}, bf16[512,12,64]{0,2,1:T(8,128)(2,1)}, u32[]{:S(2)}) copy-start(bf16[512,12,64]{0,2,1:T(8,128)(2,1)} %copy-done.14) | copy-start | bytes 2359300
  956.4 2.2 copy-start.17
  956.4 2.3 copy-start.19
  958.7 1.3 copy-start.18
Sparse Core Ops, SparseCore 0:
  11.5 56.7 all-gather.10
  71.7 52.9 all-gather.8
  128.2 52.9 all-gather.12
  184.6 52.9 all-gather.14
  240.2 39.9 all-gather.18
  303.1 27.4 all-gather.16
  333.3 41.0 all-gather.20
  381.1 36.6 reduce-scatter.14
  425.6 28.5 all-gather.22
  470.6 37.9 reduce-scatter.16
  788.1 31.9 all-reduce.8
  823.7 64.1 reduce-scatter.22
  891.7 63.0 reduce-scatter.20
  959.3 70.2 all-reduce.6
  1036.2 98.1 reduce-scatter.18
  1140.1 98.0 reduce-scatter.24
  1244.7 98.0 reduce-scatter.26
  1348.5 98.1 reduce-scatter.28
